TPU v7x, 256 devices: a whole 4x4x8 slice. The times are simulated.
256 devices in a mesh: dp: 32 (over y, x, z_lo), cam: 8 (over z_hi, core).
Axes of the slice: x: 4, y: 4, z: 8 (z_hi: 4, z_lo: 2; z = z_hi * 2 + z_lo), core: 2. Of those that a mesh axis runs over, the one named last changes fastest.
Arguments:
- grad_out: bfloat16 [32768, 3072], P(('dp', 'cam')), may hold values from -6 to 6
- query_act: bfloat16 [32768, 2048], P(('dp', 'cam')), may hold values from -13 to 13
- key_act: bfloat16 [32768, 2048], P(('dp', 'cam')), may hold values from -13 to 13
- value_act: bfloat16 [32768, 2048], P(('dp', 'cam')), may hold values from -6 to 6
- out_proj: bfloat16 [3072, 2048], P('dp'), may hold values from -0.125 to 0.125
- view_counts: int32 [32, 4], P('dp'), may hold values from 1 to 12, 16 in all within a row
- view_slots: int32 [32, 16], P('dp'), may hold values from 0 to 15, each once within a row
Outputs:
- grad_query: bfloat16 [32768, 2048], P(('dp', 'cam'))
- grad_key: bfloat16 [32768, 2048], P(('dp', 'cam'))
- grad_value: bfloat16 [32768, 2048], P(('dp', 'cam'))
- grad_proj: float32 [3072, 2048], P('dp')
Inputs may be any that keep to these rules, and one draw needn't show every extreme that they name: `view_counts`: in each group the 4 counts sum to 16, and the largest is exactly 12. `view_slots`: each row is a permutation of the group's 16 slots.
All inputs are finite; a program needn't handle non-finite values.
Results may differ from a plain program's by a relative error of at most 0.0096.
Values may be sent and summed in bfloat16 or wider, within the bound.
A program may use at most 64 MiB of HBM per device.

v0:
```python
import math
import jax
import jax.numpy as jnp
from jax import lax
from jax.sharding import PartitionSpec as P

HEAD_DIM = 128
VIEW_TOK = 64


def token_objects(counts, slots, view_tokens):
    count_ends = jnp.cumsum(counts)
    view_order = jnp.arange(slots.shape[0], dtype=jnp.int32)
    view_object = jnp.sum((view_order[:, None] >= count_ends[None, :]).astype(jnp.int32), axis=1)
    placed = slots[:, None] == view_order[None, :]
    slot_object = jnp.sum(jnp.where(placed, view_object[:, None], 0), axis=0)
    return jnp.repeat(slot_object, view_tokens)


def head_attention(query_heads, key_heads, value_heads, grad_heads, same_object, head_dim):
    group_tokens, proj_width = query_heads.shape
    head_count = proj_width // head_dim
    score_scale = 1.0 / math.sqrt(head_dim)

    def one_head(head_index):
        first_col = head_index * head_dim
        query_one = lax.dynamic_slice_in_dim(query_heads, first_col, head_dim, 1)
        key_one = lax.dynamic_slice_in_dim(key_heads, first_col, head_dim, 1)
        value_one = lax.dynamic_slice_in_dim(value_heads, first_col, head_dim, 1)
        grad_one = lax.dynamic_slice_in_dim(grad_heads, first_col, head_dim, 1)
        scores = (
            lax.dot_general(
                query_one, key_one, (((1,), (1,)), ((), ())), preferred_element_type=jnp.float32
            )
            * score_scale
        )
        scores = jnp.where(same_object, scores, -jnp.inf)
        row_max = jnp.max(scores, axis=1, keepdims=True)
        exp_scores = jnp.exp(scores - row_max)
        probs = exp_scores / jnp.sum(exp_scores, axis=1, keepdims=True)
        probs_bf16 = probs.astype(jnp.bfloat16)
        attended_f32 = jnp.dot(probs_bf16, value_one, preferred_element_type=jnp.float32)
        row_delta = jnp.sum(grad_one.astype(jnp.float32) * attended_f32, axis=1)
        grad_probs = lax.dot_general(
            grad_one, value_one, (((1,), (1,)), ((), ())), preferred_element_type=jnp.float32
        )
        grad_scores = (probs * (grad_probs - row_delta[:, None])).astype(jnp.bfloat16)
        grad_query = jnp.dot(grad_scores, key_one, preferred_element_type=jnp.float32) * score_scale
        grad_key = (
            lax.dot_general(
                grad_scores, query_one, (((0,), (0,)), ((), ())), preferred_element_type=jnp.float32
            )
            * score_scale
        )
        grad_value = lax.dot_general(
            probs_bf16, grad_one, (((0,), (0,)), ((), ())), preferred_element_type=jnp.float32
        )
        return (
            attended_f32.astype(jnp.bfloat16),
            grad_query.astype(jnp.bfloat16),
            grad_key.astype(jnp.bfloat16),
            grad_value.astype(jnp.bfloat16),
        )

    stacked = lax.map(one_head, jnp.arange(head_count, dtype=jnp.int32))

    def flatten(per_head):
        return jnp.transpose(per_head, (1, 0, 2)).reshape(group_tokens, proj_width)

    return tuple((flatten(item) for item in stacked))


def local(grad_out, query_act, key_act, value_act, out_proj, view_counts, view_slots):
    objects = token_objects(view_counts[0], view_slots[0], VIEW_TOK)
    same_object = objects[:, None] == objects[None, :]
    whole_out = lax.all_gather(grad_out, "cam", axis=0, tiled=True)
    columns = grad_out
    grad_attn = jnp.dot(
        columns,
        lax.all_gather(out_proj, "dp", axis=0, tiled=True),
        preferred_element_type=jnp.float32,
    ).astype(jnp.bfloat16)
    query_heads, key_heads, value_heads, grad_heads = (
        lax.all_to_all(query_act, "cam", split_axis=1, concat_axis=0, tiled=True),
        lax.all_to_all(key_act, "cam", split_axis=1, concat_axis=0, tiled=True),
        lax.all_to_all(value_act, "cam", split_axis=1, concat_axis=0, tiled=True),
        lax.all_to_all(grad_attn, "cam", split_axis=1, concat_axis=0, tiled=True),
    )
    attended, grad_query, grad_key, grad_value = head_attention(
        query_heads, key_heads, value_heads, grad_heads, same_object, HEAD_DIM
    )
    columns = whole_out
    partial_rows = lax.psum_scatter(
        lax.dot_general(
            columns, attended, (((0,), (0,)), ((), ())), preferred_element_type=jnp.float32
        ),
        "dp",
        scatter_dimension=0,
        tiled=True,
    )
    grad_proj = lax.all_gather(partial_rows, "cam", axis=1, tiled=True)
    grad_query, grad_key, grad_value = (
        lax.all_to_all(grad_query, "cam", split_axis=0, concat_axis=1, tiled=True),
        lax.all_to_all(grad_key, "cam", split_axis=0, concat_axis=1, tiled=True),
        lax.all_to_all(grad_value, "cam", split_axis=0, concat_axis=1, tiled=True),
    )
    return (grad_query, grad_key, grad_value, grad_proj)


def solution(mesh):
    in_specs = (
        P(("dp", "cam"), None),
        P(("dp", "cam"), None),
        P(("dp", "cam"), None),
        P(("dp", "cam"), None),
        P("dp", None),
        P("dp", None),
        P("dp", None),
    )
    out_specs = (
        P(("dp", "cam"), None),
        P(("dp", "cam"), None),
        P(("dp", "cam"), None),
        P("dp", None),
    )
    return jax.shard_map(local, mesh=mesh, in_specs=in_specs, out_specs=out_specs, check_vma=False)
```

profile of v0, /device:TPU:1, one launch (start us, length us, event | category | flops | bytes accessed | tf_op | source)
XLA Modules:
  0.0 621.5 jit_solution(6285375771550483284)
XLA Ops:
  8.7 1.9 copy.106
  10.5 10.0 %all-to-all-start = ((bf16[128,8,256]{2,0,1:T(8,128)(2,1)}), bf16[128,8,256]{2,0,1:T(8,128)(2,1)S(1)}, u32[]{:S(2)}, u32[]{:S(2)}) async-start(bf16[128,8,256]{2,0,1:T(8,128)(2,1)} %bitcast.86), calls=%async_computation | async-start | bytes 1048576 | tf_op jit(solution)/shard_map/all_to_all | solution.py:84
  20.5 1.9 copy.105
  22.4 17.7 %all-to-all-done = bf16[128,8,256]{2,0,1:T(8,128)(2,1)S(1)} async-done(((bf16[128,8,256]{2,0,1:T(8,128)(2,1)}), bf16[128,8,256]{2,0,1:T(8,128)(2,1)S(1)}, u32[]{:S(2)}, u32[]{:S(2)}) %all-to-all-start) | async-done | bytes 524320 | tf_op jit(solution)/shard_map/all_to_all | solution.py:84
  40.1 5.0 all-to-all-start.1
  45.9 22.4 %all-to-all-done.1 = bf16[128,8,256]{2,0,1:T(8,128)(2,1)S(1)} async-done(((bf16[128,8,256]{2,0,1:T(8,128)(2,1)}), bf16[128,8,256]{2,0,1:T(8,128)(2,1)S(1)}, u32[]{:S(2)}, u32[]{:S(2)}) %all-to-all-start.1) | async-done | bytes 524320 | tf_op jit(solution)/shard_map/all_to_all | solution.py:85
  68.3 4.0 all-to-all-start.2
  72.3 250.5 %all-gather.3.cloned.1.call-done = bf16[3072,2048]{1,0:T(8,128)(2,1)} async-done(((bf16[96,2048]{1,0:T(8,128)(2,1)}), bf16[3072,2048]{1,0:T(8,128)(2,1)}) %all-gather.3.cloned.1.call-update) | async-done | bytes 12582928 | tf_op jit(solution)/shard_map/all_gather | solution.py:80
  322.8 6.4 %convolution_convert_fusion.1 = bf16[128,2048]{1,0:T(8,128)(2,1)S(1)} fusion(bf16[128,3072]{1,0:T(8,128)(2,1)S(1)} %copy-done.2, bf16[3072,2048]{1,0:T(8,128)(2,1)} %all-gather.3.cloned.1.call-done), kind=kOutput, calls=%fused_computation.37 | convolution fusion | flops 1610874880 | bytes 13893632 | tf_op jit(solution)/shard_map/dot_general | solution.py:78
  330.0 6.9 %all-to-all-start.3 = ((bf16[128,8,256]{2,0,1:T(8,128)(2,1)}), bf16[128,8,256]{2,0,1:T(8,128)(2,1)S(1)}, u32[]{:S(2)}, u32[]{:S(2)}) async-start(bf16[128,8,256]{2,0,1:T(8,128)(2,1)} %bitcast.83), calls=%async_computation.3 | async-start | bytes 1048576 | tf_op jit(solution)/shard_map/all_to_all | solution.py:87
  337.5 35.0 %all-to-all-done.3 = bf16[128,8,256]{2,0,1:T(8,128)(2,1)S(1)} async-done(((bf16[128,8,256]{2,0,1:T(8,128)(2,1)}), bf16[128,8,256]{2,0,1:T(8,128)(2,1)S(1)}, u32[]{:S(2)}, u32[]{:S(2)}) %all-to-all-start.3) | async-done | bytes 524320 | tf_op jit(solution)/shard_map/all_to_all | solution.py:87
  372.5 30.3 %while.17 = (s32[]{:T(128)}, bf16[2,1024,128]{1,2,0:T(8,128)(2,1)}, bf16[2,1024,128]{2,1,0:T(8,128)(2,1)S(1)}, bf16[2,1024,128]{2,1,0:T(8,128)(2,1)}, bf16[2,102...) while((s32[]{:T(128)}, bf16[2,1024,128]{1,2,0:T(8,128)(2,1)}, ...), condition=%wide.region_7.8_spmd.clone, body=%wide.region_3.7_spmd.clone.sunk | while | flops 1631712256 | bytes 87341000 | solution.py:65
  375.5 1.4 fusion.60
  376.9 1.9 copy-done
  378.9 1.2 bitcast_dynamic-update-slice_fusion.2
  380.4 3.0 multiply_convert_fusion.2
  390.6 1.4 fusion.60
  392.0 1.9 copy-done
  394.0 1.2 bitcast_dynamic-update-slice_fusion.2
  395.5 3.0 multiply_convert_fusion.2
  403.8 4.8 convolution_bitcast_fusion
  408.6 2.4 copy.89
  411.0 1.3 copy.78
  413.3 3.7 all-to-all-start.4
  418.2 18.1 %all-to-all-done.4 = bf16[8,128,256]{1,2,0:T(8,128)(2,1)S(1)} async-done(((bf16[8,128,256]{1,2,0:T(8,128)(2,1)}), bf16[8,128,256]{1,2,0:T(8,128)(2,1)S(1)}, u32[]{:S(2)}, u32[]{:S(2)}) %all-to-all-start.4) | async-done | bytes 524320 | tf_op jit(solution)/shard_map/all_to_all | solution.py:103
  436.3 4.9 all-to-all-start.5
  442.4 20.0 %all-to-all-done.5 = bf16[8,128,256]{1,2,0:T(8,128)(2,1)S(1)} async-done(((bf16[8,128,256]{1,2,0:T(8,128)(2,1)}), bf16[8,128,256]{1,2,0:T(8,128)(2,1)S(1)}, u32[]{:S(2)}, u32[]{:S(2)}) %all-to-all-start.5) | async-done | bytes 524320 | tf_op jit(solution)/shard_map/all_to_all | solution.py:104
  462.4 4.4 all-to-all-start.6
  468.7 20.9 %all-to-all-done.6 = bf16[8,128,256]{1,2,0:T(8,128)(2,1)S(1)} async-done(((bf16[8,128,256]{1,2,0:T(8,128)(2,1)}), bf16[8,128,256]{1,2,0:T(8,128)(2,1)S(1)}, u32[]{:S(2)}, u32[]{:S(2)}) %all-to-all-start.6) | async-done | bytes 524320 | tf_op jit(solution)/shard_map/all_to_all | solution.py:105
  490.6 81.5 %reduce-scatter.4.cloned.1.call-done = f32[96,256]{1,0:T(8,128)} async-done(((f32[3072,256]{1,0:T(8,128)}), f32[96,256]{1,0:T(8,128)}) %reduce-scatter.4.cloned.1.call-update) | async-done | bytes 98320
  573.1 40.6 %all_gather.11 = f32[96,2048]{0,1:T(8,128)S(1)} all-gather(f32[96,256]{0,1:T(8,128)S(1)} %copy.90), channel_id=1, replica_groups=mesh['dp'=32,'cam'=8] {'cam'}, dimensions={1}, use_global_device_ids=true | all-gather | bytes 884736 | tf_op jit(solution)/shard_map/all_gather | solution.py:101
  613.7 1.2 copy.87
  (94 shorter events, 25.8 us)
Async XLA Ops:
  7.2 315.7 %copy-start.2 = (bf16[128,3072]{1,0:T(8,128)(2,1)S(1)}, bf16[128,3072]{1,0:T(8,128)(2,1)}, u32[]{:S(2)}) copy-start(bf16[128,3072]{1,0:T(8,128)(2,1)} %param.9) | copy-start | bytes 2359300
  7.2 37.9 %copy-start.3 = (bf16[128,2048]{1,0:T(8,128)(2,1)S(1)}, bf16[128,2048]{1,0:T(8,128)(2,1)}, u32[]{:S(2)}) copy-start(bf16[128,2048]{1,0:T(8,128)(2,1)} %param.12) | copy-start | bytes 1572868
  7.2 315.6 %all-gather.3.cloned.1.call-start = ((), (), s32[]{:S(2)}) async-start(), calls=%async_computation.8 | async-start | bytes 12976128 | tf_op jit(solution)/shard_map/all_gather | solution.py:80
  7.9 395.9 %all-gather.5.cloned.1.call-start = ((), (), s32[]{:S(2)}) async-start(), calls=%async_computation.9 | async-start | bytes 7077888 | tf_op jit(solution)/shard_map/all_gather | solution.py:76
  10.5 29.5 %all-to-all-start = ((bf16[128,8,256]{2,0,1:T(8,128)(2,1)}), bf16[128,8,256]{2,0,1:T(8,128)(2,1)S(1)}, u32[]{:S(2)}, u32[]{:S(2)}) async-start(bf16[128,8,256]{2,0,1:T(8,128)(2,1)} %bitcast.86), calls=%async_computation | async-start | bytes 1048576 | tf_op jit(solution)/shard_map/all_to_all | solution.py:84
  40.1 28.2 %all-to-all-start.1 = ((bf16[128,8,256]{2,0,1:T(8,128)(2,1)}), bf16[128,8,256]{2,0,1:T(8,128)(2,1)S(1)}, u32[]{:S(2)}, u32[]{:S(2)}) async-start(bf16[128,8,256]{2,0,1:T(8,128)(2,1)} %bitcast.85), calls=%async_computation.1 | async-start | bytes 1048576 | tf_op jit(solution)/shard_map/all_to_all | solution.py:85
  68.3 261.7 %all-to-all-start.2 = ((bf16[128,8,256]{2,0,1:T(8,128)(2,1)}), bf16[128,8,256]{2,0,1:T(8,128)(2,1)S(1)}, u32[]{:S(2)}, u32[]{:S(2)}) async-start(bf16[128,8,256]{2,0,1:T(8,128)(2,1)} %bitcast.84), calls=%async_computation.2 | async-start | bytes 1048576 | tf_op jit(solution)/shard_map/all_to_all | solution.py:86
  72.3 264.6 %copy-start.13 = (s32[1,4]{1,0:T(1,128)S(1)}, s32[1,4]{1,0:T(1,128)}, u32[]{:S(2)}) copy-start(s32[1,4]{1,0:T(1,128)} %param.14) | copy-start | bytes 52
  72.3 264.9 %copy-start.14 = (s32[1,16]{1,0:T(1,128)S(1)}, s32[1,16]{1,0:T(1,128)}, u32[]{:S(2)}) copy-start(s32[1,16]{1,0:T(1,128)} %param.15) | copy-start | bytes 196
  330.0 42.4 %all-to-all-start.3 = ((bf16[128,8,256]{2,0,1:T(8,128)(2,1)}), bf16[128,8,256]{2,0,1:T(8,128)(2,1)S(1)}, u32[]{:S(2)}, u32[]{:S(2)}) async-start(bf16[128,8,256]{2,0,1:T(8,128)(2,1)} %bitcast.83), calls=%async_computation.3 | async-start | bytes 1048576 | tf_op jit(solution)/shard_map/all_to_all | solution.py:87
  336.9 235.2 %reduce-scatter.4.cloned.1.call-start = ((), (), s32[]{:S(2)}) async-start(), calls=%async_computation.10 | async-start | bytes 3244032
  372.5 3.0 copy-start.4
  376.9 1.9 copy-start
  380.3 3.1 copy-start.7
  380.4 3.9 copy-start.5
  383.4 2.4 copy-start.1
  383.4 2.5 copy-start.10
  384.2 0.9 copy-start.8
  386.8 0.8 copy-start.11
  387.6 3.0 copy-start.4
  392.0 1.9 copy-start
  395.4 3.2 copy-start.7
  395.5 3.9 copy-start.5
  398.5 2.4 copy-start.1
  398.5 2.5 copy-start.10
  399.4 0.9 copy-start.8
  402.7 1.1 copy-start.6
  410.9 6.1 copy-start.9
  411.0 30.2 %copy-start.12 = (bf16[2,1024,128]{2,1,0:T(8,128)(2,1)S(1)}, bf16[2,1024,128]{2,1,0:T(8,128)(2,1)}, u32[]{:S(2)}) copy-start(bf16[2,1024,128]{2,1,0:T(8,128)(2,1)} %get-tuple-element.66) | copy-start | bytes 1572868
  413.3 23.0 %all-to-all-start.4 = ((bf16[8,128,256]{1,2,0:T(8,128)(2,1)}), bf16[8,128,256]{1,2,0:T(8,128)(2,1)S(1)}, u32[]{:S(2)}, u32[]{:S(2)}) async-start(bf16[8,128,256]{1,2,0:T(8,128)(2,1)} %copy.79), calls=%async_computation.4 | async-start | bytes 1048576 | tf_op jit(solution)/shard_map/all_to_all | solution.py:103
  436.3 26.1 %all-to-all-start.5 = ((bf16[8,128,256]{1,2,0:T(8,128)(2,1)}), bf16[8,128,256]{1,2,0:T(8,128)(2,1)S(1)}, u32[]{:S(2)}, u32[]{:S(2)}) async-start(bf16[8,128,256]{1,2,0:T(8,128)(2,1)} %copy.81), calls=%async_computation.5 | async-start | bytes 1048576 | tf_op jit(solution)/shard_map/all_to_all | solution.py:104
  462.4 27.3 %all-to-all-start.6 = ((bf16[8,128,256]{1,2,0:T(8,128)(2,1)}), bf16[8,128,256]{1,2,0:T(8,128)(2,1)S(1)}, u32[]{:S(2)}, u32[]{:S(2)}) async-start(bf16[8,128,256]{1,2,0:T(8,128)(2,1)} %copy.83), calls=%async_computation.6 | async-start | bytes 1048576 | tf_op jit(solution)/shard_map/all_to_all | solution.py:105
  (1 other events, 0.8 us)
Sparse Core Ops, SparseCore 0:
  9.8 312.9 all-gather.2
  324.6 79.1 all-gather.4
  411.1 161.0 reduce-scatter.3
where the time goes:
time: 622 us; the launch traced here: 621 us
  waiting for transfers between devices  469 us (75%)
  blocking collectives  40.6 us (7%)
  starting transfers between devices  38.9 us (6%)
  local copies, waits for them, and re-layouts  26.6 us (4%)
  matrix products  26.2 us (4%)
  between operations  13.9 us (2%)
    all_gather x1, waiting for transfers between devices, local(): lax.all_gather(out_proj, 'dp', axis=0, tiled=True)  250 us
    unnamed x4, waiting for transfers between devices  82.9 us
    all_gather x1, blocking collectives, local(): grad_proj = lax.all_gather(partial_rows, 'cam', axis=1, tiled=True)  40.6 us
    all_to_all x1, waiting for transfers between devices, local(): lax.all_to_all(grad_attn, 'cam', split_axis=1, concat_axis=0, tiled=True)  35 us
    all_to_all x1, waiting for transfers between devices, local(): lax.all_to_all(key_act, 'cam', split_axis=1, concat_axis=0, tiled=True)  22.4 us
    all_to_all x1, waiting for transfers between devices, local(): lax.all_to_all(grad_value, 'cam', split_axis=0, concat_axis=1, tiled=True)  20.9 us
    all_to_all x1, waiting for transfers between devices, local(): lax.all_to_all(grad_key, 'cam', split_axis=0, concat_axis=1, tiled=True)  20 us
    all_to_all x1, waiting for transfers between devices, local(): lax.all_to_all(grad_query, 'cam', split_axis=0, concat_axis=1, tiled=True)  18.1 us
  transfers between devices with their start and end apart: 10, of which 9 were waited for; matrix products, arithmetic and copies ran while one was open for 7% of the time, Pallas kernels for 0%

commit v1 on v0

--- a/solution.py
+++ b/solution.py
@@ -77,7 +77,9 @@
     columns = grad_out
     grad_attn = jnp.dot(
         columns,
-        lax.all_gather(out_proj, "dp", axis=0, tiled=True),
+        jnp.concatenate(
+            lax.all_to_all(jnp.stack([out_proj] * lax.axis_size("dp")), "dp", 0, 0), axis=0
+        ),
         preferred_element_type=jnp.float32,
     ).astype(jnp.bfloat16)
     query_heads, key_heads, value_heads, grad_heads = (

time: 622 us -> 596 us (0.958)
  waiting for transfers between devices: 469 us -> 389 us
  starting transfers between devices: 38.9 us -> 64.4 us
  blocking collectives: 40.6 us -> 61.3 us
    all_gather x1 -> x0, waiting for transfers between devices: 250 us -> none  [local(): lax.all_gather(out_proj, 'dp', axis=0, tiled=True)]
    all_to_all x1, waiting for transfers between devices: 22.4 us -> 199 us  [local(): lax.all_to_all(jnp.stack([out_proj] * lax.axis_size('dp')), 'dp', 0, 0)]
    unnamed x4 -> x3, waiting for transfers between devices: 82.9 us -> 107 us
    all_to_all x1, waiting for transfers between devices: 35 us -> 12.9 us  [local(): lax.all_to_all(grad_attn, 'cam', split_axis=1, concat_axis=0, tiled=True)]
    all_to_all x0 -> x1, blocking collectives: none -> 22 us  [local(): lax.all_to_all(key_act, 'cam', split_axis=1, concat_axis=0, tiled=True)]
    all_to_all x1, starting transfers between devices: 4.05 us -> 24 us  [local(): lax.all_to_all(value_act, 'cam', split_axis=1, concat_axis=0, tiled=True)]
    all_to_all x1, waiting for transfers between devices: 0.01 us -> 8.14 us  [local(): lax.all_to_all(value_act, 'cam', split_axis=1, concat_axis=0, tiled=True)]
  transfers between devices with their start and end apart: 10 -> 9, of which waited for: 9 -> 8; matrix products, arithmetic and copies ran while one was open for 7% -> 7% of each run, Pallas kernels for 0% -> 0%
where the time goes in v1:
time: 596 us; the launch traced here: 595 us
  waiting for transfers between devices  389 us (65%)
  starting transfers between devices  64.4 us (11%)
  blocking collectives  61.3 us (10%)
  local copies, waits for them, and re-layouts  32.2 us (5%)
  matrix products  27.1 us (5%)
  between operations  14.2 us (2%)
    all_to_all x1, waiting for transfers between devices, local(): lax.all_to_all(jnp.stack([out_proj] * lax.axis_size('dp')), 'dp', 0, 0)  199 us
    unnamed x3, waiting for transfers between devices  107 us
    all_gather x1, blocking collectives, local(): grad_proj = lax.all_gather(partial_rows, 'cam', axis=1, tiled=True)  39.3 us
    all_to_all x1, starting transfers between devices, local(): lax.all_to_all(value_act, 'cam', split_axis=1, concat_axis=0, tiled=True)  24 us
    all_to_all x1, blocking collectives, local(): lax.all_to_all(key_act, 'cam', split_axis=1, concat_axis=0, tiled=True)  22 us
    all_to_all x1, waiting for transfers between devices, local(): lax.all_to_all(grad_value, 'cam', split_axis=0, concat_axis=1, tiled=True)  18.6 us
    all_to_all x1, waiting for transfers between devices, local(): lax.all_to_all(grad_key, 'cam', split_axis=0, concat_axis=1, tiled=True)  16.9 us
    all_to_all x1, waiting for transfers between devices, local(): lax.all_to_all(grad_query, 'cam', split_axis=0, concat_axis=1, tiled=True)  14.1 us
  transfers between devices with their start and end apart: 9, of which 8 were waited for; matrix products, arithmetic and copies ran while one was open for 7% of the time, Pallas kernels for 0%

profile of v1, /device:TPU:1, one launch (start us, length us, event | category | flops | bytes accessed | tf_op | source)
XLA Modules:
  0.0 595.3 jit_solution(14426092489382381939)
XLA Ops:
  7.2 1.9 copy.106
  9.1 10.0 %all-to-all-start = ((bf16[128,8,256]{2,0,1:T(8,128)(2,1)}), bf16[128,8,256]{2,0,1:T(8,128)(2,1)S(1)}, u32[]{:S(2)}, u32[]{:S(2)}) async-start(bf16[128,8,256]{2,0,1:T(8,128)(2,1)} %bitcast.87), calls=%async_computation | async-start | bytes 1048576 | tf_op jit(solution)/shard_map/all_to_all | solution.py:86
  20.1 13.1 %all-to-all-done = bf16[128,8,256]{2,0,1:T(8,128)(2,1)S(1)} async-done(((bf16[128,8,256]{2,0,1:T(8,128)(2,1)}), bf16[128,8,256]{2,0,1:T(8,128)(2,1)S(1)}, u32[]{:S(2)}, u32[]{:S(2)}) %all-to-all-start) | async-done | bytes 524320 | tf_op jit(solution)/shard_map/all_to_all | solution.py:86
  33.2 22.0 %all_to_all.138 = bf16[128,8,256]{2,0,1:T(8,128)(2,1)S(1)} all-to-all(bf16[128,8,256]{2,0,1:T(8,128)(2,1)S(1)} %bitcast.112), channel_id=1, replica_groups=mesh['dp'=32,'cam'=8] {'cam'}, dimensions={1} | all-to-all | bytes 1048576 | tf_op jit(solution)/shard_map/all_to_all | solution.py:87
  55.2 6.1 %stack.2 = bf16[32,96,2048]{2,1,0:T(8,128)(2,1)} broadcast(bf16[96,2048]{1,0:T(8,128)(2,1)S(1)} %copy-done.8), dimensions={1,2} | broadcast | bytes 12976128 | tf_op jit(solution)/shard_map/stack | solution.py:81
  61.3 7.3 %all-to-all-start.3 = ((bf16[32,96,2048]{2,1,0:T(8,128)(2,1)}), bf16[32,96,2048]{2,1,0:T(8,128)(2,1)}, u32[]{:S(2)}, u32[]{:S(2)}) async-start(bf16[32,96,2048]{2,1,0:T(8,128)(2,1)} %stack.2), calls=%async_computation.3 | async-start | bytes 25165824 | tf_op jit(solution)/shard_map/all_to_all | solution.py:81
  70.1 199.0 %all-to-all-done.3 = bf16[32,96,2048]{2,1,0:T(8,128)(2,1)} async-done(((bf16[32,96,2048]{2,1,0:T(8,128)(2,1)}), bf16[32,96,2048]{2,1,0:T(8,128)(2,1)}, u32[]{:S(2)}, u32[]{:S(2)}) %all-to-all-start.3) | async-done | bytes 12582944 | tf_op jit(solution)/shard_map/all_to_all | solution.py:81
  269.1 24.0 %all-to-all-start.2 = ((bf16[128,8,256]{2,0,1:T(8,128)(2,1)}), bf16[128,8,256]{2,0,1:T(8,128)(2,1)S(1)}, u32[]{:S(2)}, u32[]{:S(2)}) async-start(bf16[128,8,256]{2,0,1:T(8,128)(2,1)} %bitcast.85), calls=%async_computation.2 | async-start | bytes 1048576 | tf_op jit(solution)/shard_map/all_to_all | solution.py:88
  293.1 6.4 %convolution_convert_fusion.1 = bf16[128,2048]{1,0:T(8,128)(2,1)S(1)} fusion(bf16[128,3072]{1,0:T(8,128)(2,1)S(1)} %copy-done.2, bf16[3072,2048]{1,0:T(8,128)(2,1)} %bitcast.6), kind=kOutput, calls=%fused_computation.37 | convolution fusion | flops 1610874880 | bytes 13893632 | tf_op jit(solution)/shard_map/dot_general | solution.py:78
  300.4 8.1 %all-to-all-done.2 = bf16[128,8,256]{2,0,1:T(8,128)(2,1)S(1)} async-done(((bf16[128,8,256]{2,0,1:T(8,128)(2,1)}), bf16[128,8,256]{2,0,1:T(8,128)(2,1)S(1)}, u32[]{:S(2)}, u32[]{:S(2)}) %all-to-all-start.2) | async-done | bytes 524320 | tf_op jit(solution)/shard_map/all_to_all | solution.py:88
  308.5 4.1 all-to-all-start.4
  313.1 12.9 %all-to-all-done.4 = bf16[128,8,256]{2,0,1:T(8,128)(2,1)S(1)} async-done(((bf16[128,8,256]{2,0,1:T(8,128)(2,1)}), bf16[128,8,256]{2,0,1:T(8,128)(2,1)S(1)}, u32[]{:S(2)}, u32[]{:S(2)}) %all-to-all-start.4) | async-done | bytes 524320 | tf_op jit(solution)/shard_map/all_to_all | solution.py:89
  326.0 29.8 %while.17 = (s32[]{:T(128)}, bf16[2,1024,128]{1,2,0:T(8,128)(2,1)}, bf16[2,1024,128]{2,1,0:T(8,128)(2,1)}, bf16[2,1024,128]{2,1,0:T(8,128)(2,1)S(1)}, bf16[2,102...) while((s32[]{:T(128)}, bf16[2,1024,128]{1,2,0:T(8,128)(2,1)}, ...), condition=%wide.region_7.8_spmd.clone, body=%wide.region_3.7_spmd.clone.sunk | while | flops 1631712256 | bytes 83147144 | solution.py:65
  329.2 1.4 fusion.60
  330.6 1.9 copy-done
  334.1 3.0 multiply_convert_fusion.2
  338.0 1.5 fusion.61
  339.5 1.4 fusion.63
  345.5 1.9 copy-done
  349.0 3.0 multiply_convert_fusion.2
  352.8 1.5 fusion.61
  354.3 1.4 fusion.63
  356.6 4.8 convolution_bitcast_fusion
  361.3 2.3 copy.89
  366.0 8.4 %all-to-all-start.5 = ((bf16[8,128,256]{1,2,0:T(8,128)(2,1)}), bf16[8,128,256]{1,2,0:T(8,128)(2,1)S(1)}, u32[]{:S(2)}, u32[]{:S(2)}) async-start(bf16[8,128,256]{1,2,0:T(8,128)(2,1)} %copy.79), calls=%async_computation.5 | async-start | bytes 1048576 | tf_op jit(solution)/shard_map/all_to_all | solution.py:105
  375.6 14.1 %all-to-all-done.5 = bf16[8,128,256]{1,2,0:T(8,128)(2,1)S(1)} async-done(((bf16[8,128,256]{1,2,0:T(8,128)(2,1)}), bf16[8,128,256]{1,2,0:T(8,128)(2,1)S(1)}, u32[]{:S(2)}, u32[]{:S(2)}) %all-to-all-start.5) | async-done | bytes 524320 | tf_op jit(solution)/shard_map/all_to_all | solution.py:105
  389.7 5.8 all-to-all-start.6
  397.8 16.9 %all-to-all-done.6 = bf16[8,128,256]{1,2,0:T(8,128)(2,1)S(1)} async-done(((bf16[8,128,256]{1,2,0:T(8,128)(2,1)}), bf16[8,128,256]{1,2,0:T(8,128)(2,1)S(1)}, u32[]{:S(2)}, u32[]{:S(2)}) %all-to-all-start.6) | async-done | bytes 524320 | tf_op jit(solution)/shard_map/all_to_all | solution.py:106
  414.6 4.8 all-to-all-start.7
  421.4 18.6 %all-to-all-done.7 = bf16[8,128,256]{1,2,0:T(8,128)(2,1)S(1)} async-done(((bf16[8,128,256]{1,2,0:T(8,128)(2,1)}), bf16[8,128,256]{1,2,0:T(8,128)(2,1)S(1)}, u32[]{:S(2)}, u32[]{:S(2)}) %all-to-all-start.7) | async-done | bytes 524320 | tf_op jit(solution)/shard_map/all_to_all | solution.py:107
  441.1 105.9 %reduce-scatter.4.cloned.1.call-done = f32[96,256]{1,0:T(8,128)} async-done(((f32[3072,256]{1,0:T(8,128)}), f32[96,256]{1,0:T(8,128)}) %reduce-scatter.4.cloned.1.call-update) | async-done | bytes 98320
  547.9 39.3 %all_gather.7 = f32[96,2048]{0,1:T(8,128)S(1)} all-gather(f32[96,256]{0,1:T(8,128)S(1)} %copy.90), channel_id=1, replica_groups=mesh['dp'=32,'cam'=8] {'cam'}, dimensions={1}, use_global_device_ids=true | all-gather | bytes 884736 | tf_op jit(solution)/shard_map/all_gather | solution.py:103
  (85 shorter events, 26.9 us)
Async XLA Ops:
  7.2 48.0 %copy-start.8 = (bf16[96,2048]{1,0:T(8,128)(2,1)S(1)}, bf16[96,2048]{1,0:T(8,128)(2,1)}, u32[]{:S(2)}) copy-start(bf16[96,2048]{1,0:T(8,128)(2,1)} %param.13) | copy-start | bytes 1179652
  9.1 24.1 %all-to-all-start = ((bf16[128,8,256]{2,0,1:T(8,128)(2,1)}), bf16[128,8,256]{2,0,1:T(8,128)(2,1)S(1)}, u32[]{:S(2)}, u32[]{:S(2)}) async-start(bf16[128,8,256]{2,0,1:T(8,128)(2,1)} %bitcast.87), calls=%async_computation | async-start | bytes 1048576 | tf_op jit(solution)/shard_map/all_to_all | solution.py:86
  61.3 8.0 %copy-start.3 = (bf16[128,2048]{1,0:T(8,128)(2,1)S(1)}, bf16[128,2048]{1,0:T(8,128)(2,1)}, u32[]{:S(2)}) copy-start(bf16[128,2048]{1,0:T(8,128)(2,1)} %param.12) | copy-start | bytes 1572868
  61.3 231.9 %copy-start.2 = (bf16[128,3072]{1,0:T(8,128)(2,1)S(1)}, bf16[128,3072]{1,0:T(8,128)(2,1)}, u32[]{:S(2)}) copy-start(bf16[128,3072]{1,0:T(8,128)(2,1)} %param.9) | copy-start | bytes 2359300
  61.3 207.8 %all-to-all-start.3 = ((bf16[32,96,2048]{2,1,0:T(8,128)(2,1)}), bf16[32,96,2048]{2,1,0:T(8,128)(2,1)}, u32[]{:S(2)}, u32[]{:S(2)}) async-start(bf16[32,96,2048]{2,1,0:T(8,128)(2,1)} %stack.2), calls=%async_computation.3 | async-start | bytes 25165824 | tf_op jit(solution)/shard_map/all_to_all | solution.py:81
  68.6 287.2 %all-gather.2.cloned.1.call-start = ((), (), s32[]{:S(2)}) async-start(), calls=%async_computation.9 | async-start | bytes 7077888 | tf_op jit(solution)/shard_map/all_gather | solution.py:76
  269.1 39.4 %all-to-all-start.2 = ((bf16[128,8,256]{2,0,1:T(8,128)(2,1)}), bf16[128,8,256]{2,0,1:T(8,128)(2,1)S(1)}, u32[]{:S(2)}, u32[]{:S(2)}) async-start(bf16[128,8,256]{2,0,1:T(8,128)(2,1)} %bitcast.85), calls=%async_computation.2 | async-start | bytes 1048576 | tf_op jit(solution)/shard_map/all_to_all | solution.py:88
  293.1 19.5 %copy-start.11 = (s32[1,4]{1,0:T(1,128)S(1)}, s32[1,4]{1,0:T(1,128)}, u32[]{:S(2)}) copy-start(s32[1,4]{1,0:T(1,128)} %param.14) | copy-start | bytes 52
  293.1 19.8 %copy-start.12 = (s32[1,16]{1,0:T(1,128)S(1)}, s32[1,16]{1,0:T(1,128)}, u32[]{:S(2)}) copy-start(s32[1,16]{1,0:T(1,128)} %param.15) | copy-start | bytes 196
  308.5 17.5 %all-to-all-start.4 = ((bf16[128,8,256]{2,0,1:T(8,128)(2,1)}), bf16[128,8,256]{2,0,1:T(8,128)(2,1)S(1)}, u32[]{:S(2)}, u32[]{:S(2)}) async-start(bf16[128,8,256]{2,0,1:T(8,128)(2,1)} %bitcast.84), calls=%async_computation.4 | async-start | bytes 1048576 | tf_op jit(solution)/shard_map/all_to_all | solution.py:89
  312.6 234.3 %reduce-scatter.4.cloned.1.call-start = ((), (), s32[]{:S(2)}) async-start(), calls=%async_computation.10 | async-start | bytes 3244032
  326.0 3.1 copy-start.4
  329.2 3.4 copy-start.9
  330.6 2.0 copy-start
  333.1 0.8 copy-start.10
  334.1 3.8 copy-start.5
  337.1 2.4 copy-start.1
  340.9 3.1 copy-start.4
  344.0 3.4 copy-start.9
  345.5 2.0 copy-start
  347.9 0.8 copy-start.10
  349.0 3.9 copy-start.5
  352.0 2.4 copy-start.1
  355.8 0.8 copy-start.6
  363.7 10.7 %copy-start.7 = (bf16[2,1024,128]{2,1,0:T(8,128)(2,1)S(1)}, bf16[2,1024,128]{2,1,0:T(8,128)(2,1)}, u32[]{:S(2)}) copy-start(bf16[2,1024,128]{2,1,0:T(8,128)(2,1)} %copy-done.6) | copy-start | bytes 1572868
  366.0 23.7 %all-to-all-start.5 = ((bf16[8,128,256]{1,2,0:T(8,128)(2,1)}), bf16[8,128,256]{1,2,0:T(8,128)(2,1)S(1)}, u32[]{:S(2)}, u32[]{:S(2)}) async-start(bf16[8,128,256]{1,2,0:T(8,128)(2,1)} %copy.79), calls=%async_computation.5 | async-start | bytes 1048576 | tf_op jit(solution)/shard_map/all_to_all | solution.py:105
  389.7 24.9 %all-to-all-start.6 = ((bf16[8,128,256]{1,2,0:T(8,128)(2,1)}), bf16[8,128,256]{1,2,0:T(8,128)(2,1)S(1)}, u32[]{:S(2)}, u32[]{:S(2)}) async-start(bf16[8,128,256]{1,2,0:T(8,128)(2,1)} %copy.81), calls=%async_computation.6 | async-start | bytes 1048576 | tf_op jit(solution)/shard_map/all_to_all | solution.py:106
  414.6 25.4 %all-to-all-start.7 = ((bf16[8,128,256]{1,2,0:T(8,128)(2,1)}), bf16[8,128,256]{1,2,0:T(8,128)(2,1)S(1)}, u32[]{:S(2)}, u32[]{:S(2)}) async-start(bf16[8,128,256]{1,2,0:T(8,128)(2,1)} %copy.83), calls=%async_computation.7 | async-start | bytes 1048576 | tf_op jit(solution)/shard_map/all_to_all | solution.py:107
Sparse Core Ops, SparseCore 0:
  71.2 95.8 all-gather.1
  363.8 183.0 reduce-scatter.3
